TPU v7x, 32 devices: a whole 2x2x4 slice. The times are simulated.
32 devices in a mesh: fsdp: 8 (over z, y), seq: 4 (over x, core).
Axes of the slice: x: 2, y: 2, z: 4, core: 2. Of those that a mesh axis runs over, the one named last changes fastest.
Arguments:
- tokens: bfloat16 [16, 1024, 1024], P('fsdp', 'seq'), may hold values from -6 to 6
- first_gain: float32 [1024], replicated, may hold values from 0.5 to 1.5
- first_shift: float32 [1024], replicated, may hold values from -1 to 1
- attention_weight: bfloat16 [1024, 3072], P('fsdp', 'seq'), may hold values from -0.25 to 0.25
- attention_bias: float32 [3072], replicated, may hold values from -1.5 to 1.5
- output_weight: bfloat16 [1024, 1024], P('fsdp', 'seq'), may hold values from -1.5 to 1.5
- output_bias: float32 [1024], replicated, may hold values from -1 to 1
- second_gain: float32 [1024], replicated, may hold values from 0.5 to 1.5
- second_shift: float32 [1024], replicated, may hold values from -1 to 1
- expand_weight: bfloat16 [1024, 4096], P('fsdp', 'seq'), may hold values from -0.1875 to 0.1875
- expand_bias: float32 [4096], replicated, may hold values from -1 to 1
- contract_weight: bfloat16 [4096, 1024], P('fsdp', 'seq'), may hold values from -0.1875 to 0.1875
- contract_bias: float32 [1024], replicated, may hold values from -1 to 1
- cotangent: bfloat16 [16, 1024, 1024], P('fsdp', 'seq'), may hold values from -6 to 6
- threshold: float32 [1], replicated, may hold values from 3 to 6
Outputs:
- block_output: bfloat16 [16, 1024, 1024], P('fsdp', 'seq')
- input_grad: float32 [16, 1024, 1024], P('fsdp', 'seq')
- grad_first_gain: float32 [1024], replicated
- grad_first_shift: float32 [1024], replicated
- grad_attention_weight: float32 [1024, 3072], P('fsdp', 'seq')
- grad_attention_bias: float32 [3072], replicated
- grad_output_weight: float32 [1024, 1024], P('fsdp', 'seq')
- grad_output_bias: float32 [1024], replicated
- grad_second_gain: float32 [1024], replicated
- grad_second_shift: float32 [1024], replicated
- grad_expand_weight: float32 [1024, 4096], P('fsdp', 'seq')
- grad_expand_bias: float32 [4096], replicated
- grad_contract_weight: float32 [4096, 1024], P('fsdp', 'seq')
- grad_contract_bias: float32 [1024], replicated
- head_peak: float32 [16], P('seq')
- clipped_weight: float32 [1024, 3072], P('fsdp', 'seq')
- clipped_bias: float32 [3072], P('seq')
All inputs are finite; a program needn't handle non-finite values.
Results may differ from a plain program's by a relative error of at most 0.018.
Values may be sent and summed in bfloat16 or wider, within the bound.
No kernel may reach another device: no remote copies, remote signals or barrier semaphores. Data moves between devices by JAX's collectives and lax.ppermute only.
A program may use at most 320 MiB of HBM per device.

v0:
```python
import jax
import jax.numpy as jnp
from jax import lax
from jax.sharding import PartitionSpec as P

D = 1024
H = 16
HD = 64
QBLK = 512


def layer_norm(values, gain, shift):
    centered = values - jnp.mean(values, axis=-1, keepdims=True)
    variance = jnp.mean(centered * centered, axis=-1, keepdims=True)
    return centered * lax.rsqrt(variance + 1e-05) * gain + shift


def gelu_tanh(values):
    return jax.nn.gelu(values, approximate=True)


def causal_mask(row_start, row_stop):
    row_ids = row_start + jnp.arange(row_stop - row_start)[:, None]
    col_ids = jnp.arange(row_stop)[None, :]
    return col_ids <= row_ids


def block_logits(query_block, keys_part, row_start, row_stop, logit_scale):
    logits = (
        jnp.einsum("nqhd,nkhd->nhqk", query_block, keys_part, preferred_element_type=jnp.float32)
        * logit_scale
    )
    return jnp.where(causal_mask(row_start, row_stop), logits, -jnp.inf)


def split_packed(packed):
    head_size = packed.shape[-1] // 3
    return (
        packed[..., :head_size],
        packed[..., head_size : 2 * head_size],
        packed[..., 2 * head_size :],
    )


def attend_forward(packed):
    queries, keys_all, values_all = split_packed(packed)
    length = packed.shape[1]
    logit_scale = queries.shape[-1] ** (-0.5)
    outputs = []
    log_sums = []
    peak_value = None
    for block_index in range(length // QBLK):
        row_start = block_index * QBLK
        row_stop = row_start + QBLK
        logits = block_logits(
            queries[:, row_start:row_stop], keys_all[:, :row_stop], row_start, row_stop, logit_scale
        )
        row_top = jnp.max(logits, axis=-1, keepdims=True)
        shifted = jnp.exp(logits - row_top)
        row_total = jnp.sum(shifted, axis=-1, keepdims=True)
        probabilities = (shifted / row_total).astype(jnp.bfloat16)
        block_out = jnp.einsum(
            "nhqk,nkhd->nqhd",
            probabilities,
            values_all[:, :row_stop],
            preferred_element_type=jnp.float32,
        )
        outputs.append(block_out.astype(jnp.bfloat16))
        log_sums.append((row_top + jnp.log(row_total))[..., 0])
        block_peak = jnp.max(row_top[..., 0], axis=-1)
        peak_value = block_peak if peak_value is None else jnp.maximum(peak_value, block_peak)
    return (jnp.concatenate(outputs, axis=1), jnp.concatenate(log_sums, axis=-1), peak_value)


def attend_items(packed):
    attended, log_sums, peak_value = attend_forward(packed)
    returned = lax.all_to_all(attended, "seq", split_axis=1, concat_axis=2, tiled=True)
    return (returned, log_sums, peak_value, packed)


def attend_backward(packed, log_sums, heads_cot):
    queries, keys_all, values_all = split_packed(packed)
    length = packed.shape[1]
    logit_scale = queries.shape[-1] ** (-0.5)
    query_grads = []
    key_grad = jnp.zeros(keys_all.shape, jnp.float32)
    value_grad = jnp.zeros(values_all.shape, jnp.float32)
    for block_index in range(length // QBLK):
        row_start = block_index * QBLK
        row_stop = row_start + QBLK
        query_block = queries[:, row_start:row_stop]
        cot_block = heads_cot[:, row_start:row_stop]
        logits = block_logits(query_block, keys_all[:, :row_stop], row_start, row_stop, logit_scale)
        probabilities = jnp.exp(logits - log_sums[:, :, row_start:row_stop, None])
        prob_grad = jnp.einsum(
            "nqhd,nkhd->nhqk",
            cot_block,
            values_all[:, :row_stop],
            preferred_element_type=jnp.float32,
        )
        row_inner = jnp.sum(prob_grad * probabilities, axis=-1, keepdims=True)
        logit_grad = (probabilities * (prob_grad - row_inner)).astype(jnp.bfloat16)
        query_grads.append(
            jnp.einsum(
                "nhqk,nkhd->nqhd",
                logit_grad,
                keys_all[:, :row_stop],
                preferred_element_type=jnp.float32,
            )
            * logit_scale
        )
        key_grad = key_grad.at[:, :row_stop].add(
            jnp.einsum(
                "nhqk,nqhd->nkhd", logit_grad, query_block, preferred_element_type=jnp.float32
            )
            * logit_scale
        )
        value_grad = value_grad.at[:, :row_stop].add(
            jnp.einsum(
                "nhqk,nqhd->nkhd",
                probabilities.astype(jnp.bfloat16),
                cot_block,
                preferred_element_type=jnp.float32,
            )
        )
    joined = jnp.concatenate([jnp.concatenate(query_grads, axis=1), key_grad, value_grad], axis=-1)
    return joined.astype(jnp.bfloat16)


def body(
    tokens,
    first_gain,
    first_shift,
    attention_weight,
    attention_bias,
    output_weight,
    output_bias,
    second_gain,
    second_shift,
    expand_weight,
    expand_bias,
    contract_weight,
    contract_bias,
    cotangent,
    threshold,
):
    partial_full = (
        lax.all_gather(attention_weight, "seq", axis=1, tiled=True),
        lax.all_gather(output_weight, "seq", axis=1, tiled=True),
        lax.all_gather(expand_weight, "seq", axis=1, tiled=True),
        lax.all_gather(contract_weight, "seq", axis=1, tiled=True),
    )
    full_weights = (
        lax.all_gather(partial_full[0], "fsdp", axis=0, tiled=True),
        lax.all_gather(partial_full[1], "fsdp", axis=0, tiled=True),
        lax.all_gather(partial_full[2], "fsdp", axis=0, tiled=True),
        lax.all_gather(partial_full[3], "fsdp", axis=0, tiled=True),
    )
    mixing_full, output_full, expand_full, contract_full = full_weights
    seq_here = tokens.shape[0]
    tok_here = tokens.shape[1]
    tokens_float = tokens.astype(jnp.float32)
    normed_first = layer_norm(tokens_float, first_gain, first_shift).astype(jnp.bfloat16)
    mixed = (
        jnp.einsum("ntd,de->nte", normed_first, mixing_full, preferred_element_type=jnp.float32)
        + attention_bias
    )
    mixed = mixed.astype(jnp.bfloat16).reshape(seq_here, tok_here, H, 3 * HD)
    returned, log_sums, peaks, packed = attend_items(
        lax.all_to_all(mixed, "seq", split_axis=2, concat_axis=1, tiled=True)
    )
    attended = returned.reshape(seq_here, tok_here, D)
    residual = (
        tokens_float
        + jnp.einsum("nte,ed->ntd", attended, output_full, preferred_element_type=jnp.float32)
        + output_bias
    )
    normed_second = layer_norm(residual, second_gain, second_shift).astype(jnp.bfloat16)
    hidden = (
        jnp.einsum("ntd,di->nti", normed_second, expand_full, preferred_element_type=jnp.float32)
        + expand_bias
    )
    active = gelu_tanh(hidden).astype(jnp.bfloat16)
    result = (
        residual
        + jnp.einsum("nti,id->ntd", active, contract_full, preferred_element_type=jnp.float32)
        + contract_bias
    )
    block_output = result.astype(jnp.bfloat16)
    cot_float = cotangent.astype(jnp.float32)
    grad_contract = jnp.einsum("nti,ntd->id", active, cotangent, preferred_element_type=jnp.float32)
    grad_contract_bias = jnp.sum(cot_float, axis=(0, 1))
    active_cot = jnp.einsum(
        "ntd,id->nti", cotangent, contract_full, preferred_element_type=jnp.float32
    )
    _, gelu_pull = jax.vjp(gelu_tanh, hidden)
    hidden_cot = gelu_pull(active_cot)[0].astype(jnp.bfloat16)
    grad_expand = jnp.einsum(
        "ntd,nti->di", normed_second, hidden_cot, preferred_element_type=jnp.float32
    )
    grad_expand_bias = jnp.sum(hidden_cot.astype(jnp.float32), axis=(0, 1))
    second_cot = jnp.einsum(
        "nti,di->ntd", hidden_cot, expand_full, preferred_element_type=jnp.float32
    )
    _, second_pull = jax.vjp(layer_norm, residual, second_gain, second_shift)
    residual_part, grad_second_gain, grad_second_shift = second_pull(second_cot)
    residual_cot = cot_float + residual_part
    branch_cot = residual_cot.astype(jnp.bfloat16)
    grad_output = jnp.einsum(
        "nte,ntd->ed", attended, branch_cot, preferred_element_type=jnp.float32
    )
    grad_output_bias = jnp.sum(branch_cot.astype(jnp.float32), axis=(0, 1))
    attended_cot = jnp.einsum(
        "ntd,ed->nte", branch_cot, output_full, preferred_element_type=jnp.float32
    )
    attended_cot = attended_cot.astype(jnp.bfloat16).reshape(seq_here, tok_here, H, HD)
    heads_cot = lax.all_to_all(attended_cot, "seq", split_axis=2, concat_axis=1, tiled=True)
    packed_cot = attend_backward(packed, log_sums, heads_cot)
    mixed_cot = lax.all_to_all(packed_cot, "seq", split_axis=1, concat_axis=2, tiled=True).reshape(
        seq_here, tok_here, 3 * D
    )
    grad_mixing = jnp.einsum(
        "ntd,nte->de", normed_first, mixed_cot, preferred_element_type=jnp.float32
    )
    grad_mixing_bias = jnp.sum(mixed_cot.astype(jnp.float32), axis=(0, 1))
    first_cot = jnp.einsum(
        "nte,de->ntd", mixed_cot, mixing_full, preferred_element_type=jnp.float32
    )
    _, first_pull = jax.vjp(layer_norm, tokens_float, first_gain, first_shift)
    token_part, grad_first_gain, grad_first_shift = first_pull(first_cot)
    input_grad = residual_cot + token_part
    summed_first = (
        lax.psum_scatter(
            grad_mixing.astype(jnp.bfloat16), "fsdp", scatter_dimension=0, tiled=True
        ).astype(jnp.float32),
        lax.psum_scatter(
            grad_output.astype(jnp.bfloat16), "fsdp", scatter_dimension=0, tiled=True
        ).astype(jnp.float32),
        lax.psum_scatter(
            grad_expand.astype(jnp.bfloat16), "fsdp", scatter_dimension=0, tiled=True
        ).astype(jnp.float32),
        lax.psum_scatter(
            grad_contract.astype(jnp.bfloat16), "fsdp", scatter_dimension=0, tiled=True
        ).astype(jnp.float32),
    )
    weight_grads = (
        lax.psum_scatter(
            summed_first[0].astype(jnp.bfloat16), "seq", scatter_dimension=1, tiled=True
        ).astype(jnp.float32),
        lax.psum_scatter(
            summed_first[1].astype(jnp.bfloat16), "seq", scatter_dimension=1, tiled=True
        ).astype(jnp.float32),
        lax.psum_scatter(
            summed_first[2].astype(jnp.bfloat16), "seq", scatter_dimension=1, tiled=True
        ).astype(jnp.float32),
        lax.psum_scatter(
            summed_first[3].astype(jnp.bfloat16), "seq", scatter_dimension=1, tiled=True
        ).astype(jnp.float32),
    )
    vector_totals = lax.psum(
        (
            grad_first_gain,
            grad_first_shift,
            grad_mixing_bias,
            grad_output_bias,
            grad_second_gain,
            grad_second_shift,
            grad_expand_bias,
            grad_contract_bias,
        ),
        ("fsdp", "seq"),
    )
    head_peak = lax.pmax(jnp.max(peaks, axis=0), "fsdp")
    rows_here = attention_weight.shape[0]
    col_width = attention_weight.shape[1]
    heads_here = head_peak.shape[0]
    head_size = col_width // (3 * heads_here)
    factor = jnp.sqrt(threshold[0] / jnp.maximum(head_peak, threshold[0]))
    multiplier = jnp.stack([factor, factor, jnp.ones_like(factor)], axis=1)
    clipped_weight = (
        attention_weight.astype(jnp.float32).reshape(rows_here, heads_here, 3, head_size)
        * multiplier[None, :, :, None]
    ).reshape(rows_here, col_width)
    bias_piece = lax.dynamic_slice_in_dim(
        attention_bias, lax.axis_index("seq") * col_width, col_width
    )
    clipped_bias = (bias_piece.reshape(heads_here, 3, head_size) * multiplier[:, :, None]).reshape(
        col_width
    )
    return (
        block_output,
        input_grad,
        vector_totals[0],
        vector_totals[1],
        weight_grads[0],
        vector_totals[2],
        weight_grads[1],
        vector_totals[3],
        vector_totals[4],
        vector_totals[5],
        weight_grads[2],
        vector_totals[6],
        weight_grads[3],
        vector_totals[7],
        head_peak,
        clipped_weight,
        clipped_bias,
    )


def solution(mesh):
    placed = (
        P("fsdp", "seq", None),
        P(),
        P(),
        P("fsdp", "seq"),
        P(),
        P("fsdp", "seq"),
        P(),
        P(),
        P(),
        P("fsdp", "seq"),
        P(),
        P("fsdp", "seq"),
        P(),
        P("fsdp", "seq", None),
        P(),
    )
    return jax.shard_map(
        body,
        mesh=mesh,
        in_specs=placed,
        out_specs=(
            P("fsdp", "seq", None),
            P("fsdp", "seq", None),
            P(),
            P(),
            P("fsdp", "seq"),
            P(),
            P("fsdp", "seq"),
            P(),
            P(),
            P(),
            P("fsdp", "seq"),
            P(),
            P("fsdp", "seq"),
            P(),
            P("seq"),
            P("fsdp", "seq"),
            P("seq"),
        ),
        check_vma=False,
    )
```

profile of v0, /device:TPU:0, one launch (start us, length us, event | category | flops | bytes accessed | tf_op | source)
XLA Modules:
  0.0 1167.2 jit_solution(12801582693143362905)
XLA Ops:
  8.8 11.7 %all_gather.24 = bf16[128,3072]{1,0:T(8,128)(2,1)} all-gather(bf16[128,768]{1,0:T(8,128)(2,1)} %param.30), channel_id=1, replica_groups=mesh['fsdp'=8,'seq'=4] {'seq'}, dimensions={1}, use_global_device_ids=true | all-gather | bytes 983040 | tf_op jit(solution)/shard_map/all_gather | solution.py:148
  20.5 8.3 all_gather.26
  30.6 18.4 %all-gather.15.cloned.1.call-done = bf16[512,1024]{1,0:T(8,128)(2,1)} async-done(((bf16[512,256]{1,0:T(8,128)(2,1)}), bf16[512,1024]{1,0:T(8,128)(2,1)}) %all-gather.15.cloned.1.call-update) | async-done | bytes 1048592 | tf_op jit(solution)/shard_map/all_gather | solution.py:151
  49.6 100.5 %all-gather.7.cloned.1.call-done = bf16[1024,3072]{1,0:T(8,128)(2,1)} async-done(((bf16[128,3072]{1,0:T(8,128)(2,1)}), bf16[1024,3072]{1,0:T(8,128)(2,1)}) %all-gather.7.cloned.1.call-update) | async-done | bytes 6291472 | tf_op jit(solution)/shard_map/all_gather | solution.py:154
  150.2 7.8 add_convert_fusion
  172.2 36.5 %all-to-all-done = bf16[2,256,16,192]{1,3,0,2:T(8,128)(2,1)} async-done(((bf16[2,256,16,192]{1,3,0,2:T(8,128)(2,1)}), bf16[2,256,16,192]{1,3,0,2:T(8,128)(2,1)}, u32[]{:S(2)}, u32[]{:S(2)}) %all-to-all-start) | async-done | bytes 3145760 | tf_op jit(solution)/shard_map/all_to_all | solution.py:170
  208.7 6.3 copy.158
  248.0 18.9 %all_to_all.66 = bf16[4,2,65536]{2,1,0:T(2,128)(2,1)} all-to-all(bf16[4,2,65536]{2,1,0:T(2,128)(2,1)} %reshape.309), channel_id=1, replica_groups=mesh['fsdp'=8,'seq'=4] {'seq'}, dimensions={0} | all-to-all | bytes 2097152 | tf_op jit(solution)/shard_map/all_to_all | solution.py:77
  276.3 48.9 %all-gather.13.cloned.1.call-done = bf16[1024,4096]{1,0:T(8,128)(2,1)} async-done(((bf16[128,4096]{1,0:T(8,128)(2,1)}), bf16[1024,4096]{1,0:T(8,128)(2,1)}) %all-gather.13.cloned.1.call-update) | async-done | bytes 8388624 | tf_op jit(solution)/shard_map/all_gather | solution.py:156
  325.2 10.2 fusion.17
  335.4 114.9 %all-gather.17.cloned.1.call-done = bf16[4096,1024]{1,0:T(8,128)(2,1)} async-done(((bf16[512,1024]{1,0:T(8,128)(2,1)}), bf16[4096,1024]{1,0:T(8,128)(2,1)}) %all-gather.17.cloned.1.call-update) | async-done | bytes 8388624 | tf_op jit(solution)/shard_map/all_gather | solution.py:157
  450.4 14.6 %convert_reduce_fusion = (f32[4096]{0:T(1024)}, bf16[2,256,4096]{2,1,0:T(8,128)(2,1)S(1)}) fusion(f32[2,256,4096]{2,1,0:T(8,128)} %fusion.17, f32[4096]{0:T(1024)S(1)} %copy-done.41, bf16[2,256,1024]{2,1,0:T(8,128)(2,1)} %param.40, bf16[4096,1024]{1,0:T(8,128)(2,1)} %all-gather.17.cloned.1.call-done), kind=kOutput, calls=%fused_computation.29 | convolution fusion | flops 4343197696 | bytes 22052864 | tf_op jit(solution)/shard_map/ntd,id->nti/dot_general | solution.py:193
  486.9 9.9 all-to-all-done.2
  506.7 7.6 fusion.99
  526.2 10.9 fusion.98
  537.1 7.9 multiply_convert_fusion
  560.0 7.6 copy.170
  567.6 53.8 %all_to_all.67 = bf16[2,1024,4,192]{3,2,0,1:T(4,128)(2,1)} all-to-all(bf16[2,1024,4,192]{3,2,0,1:T(4,128)(2,1)} %copy.170), channel_id=1, replica_groups=mesh['fsdp'=8,'seq'=4] {'seq'}, dimensions={1} | all-to-all | bytes 6291456 | tf_op jit(solution)/shard_map/all_to_all | solution.py:219
  621.5 7.3 copy.172
  628.7 7.7 bitcast_convert_fusion.2
  637.7 13.1 %bitcast_convert_fusion = bf16[4096,1024]{1,0:T(8,128)(2,1)} fusion(bf16[2,256,1024]{2,1,0:T(8,128)(2,1)S(1)} %copy-done.12, f32[2,256,4096]{2,1,0:T(8,128)} %fusion.17, f32[4096]{0:T(1024)S(1)} %copy-done.42), kind=kOutput, calls=%fused_computation | convolution fusion | flops 4320133120 | bytes 17842176 | tf_op jit(solution)/shard_map/nti,ntd->id/dot_general | solution.py:191
  652.4 9.5 bitcast_convert_fusion.1
  662.7 89.2 %reduce-scatter.9.cloned.1.call-done = bf16[128,3072]{1,0:T(8,128)(2,1)} async-done(((bf16[1024,3072]{1,0:T(8,128)(2,1)}), bf16[128,3072]{1,0:T(8,128)(2,1)}) %reduce-scatter.9.cloned.1.call-update) | async-done | bytes 786448 | tf_op jit(solution)/shard_map/reduce_scatter | solution.py:233
  752.7 151.0 %reduce-scatter.21.cloned.1.call-done = bf16[512,1024]{1,0:T(8,128)(2,1)} async-done(((bf16[4096,1024]{1,0:T(8,128)(2,1)}), bf16[512,1024]{1,0:T(8,128)(2,1)}) %reduce-scatter.21.cloned.1.call-update) | async-done | bytes 1048592 | tf_op jit(solution)/shard_map/reduce_scatter | solution.py:242
  903.8 12.2 %add_convert_fusion.1 = bf16[2,256,1024]{2,1,0:T(8,128)(2,1)} fusion(f32[2,256,1024]{2,1,0:T(8,128)S(1)} %copy-done.6, bf16[4096,1024]{1,0:T(8,128)(2,1)} %all-gather.17.cloned.1.call-done, f32[1024]{0:T(1024)S(1)} %copy-done.47, f32[2,256,4096]{2,1,0:T(8,128)} %fusion.17, f32[4096]{0:T(1024)S(1)} %copy-done.42), kind=kOutput, calls=%fused_computation.83 | convolution fusion | flops 4317511680 | bytes 19943424 | tf_op jit(solution)/shard_map/nti,id->ntd/dot_general | solution.py:186
  916.0 20.6 %pmax.7 = f32[4]{0:T(128)S(1)} all-reduce(f32[4]{0:T(128)S(1)} %maximum_reduce_fusion), channel_id=1, replica_groups=mesh['fsdp'=8,'seq'=4] {'fsdp'}, use_global_device_ids=true, to_apply=%region_41.42 | all-reduce | flops 4 | bytes 32 | tf_op jit(solution)/shard_map/pmax | solution.py:273
  939.2 8.0 copy.193
  950.7 105.3 %reduce-scatter.17.cloned.1.call-done = bf16[128,4096]{1,0:T(8,128)(2,1)} async-done(((bf16[1024,4096]{1,0:T(8,128)(2,1)}), bf16[128,4096]{1,0:T(8,128)(2,1)}) %reduce-scatter.17.cloned.1.call-update) | async-done | bytes 1048592 | tf_op jit(solution)/shard_map/reduce_scatter | solution.py:239
  1056.0 7.0 fusion.100
  1066.7 40.8 %all-reduce.2 = (f32[1024]{0:T(1024)}, f32[1024]{0:T(1024)}, f32[3072]{0:T(1024)}, f32[1024]{0:T(1024)}, f32[1024]{0:T(1024)}, /*index=5*/f32[1024]{0:T(1024)}, f32[4096]{0:T(1024)}, f32[1024]{0:T(1024)}) all-reduce(f32[1024]{0:T(1024)S(1)} %get-tuple-element.87, ...), channel_id=1, replica_groups=mesh['fsdp'=8,'seq'=4] {'fsdp','seq'}, use_global_device_ids=true, to_apply=%region_15.16 | all-reduce | flops 13312 | bytes 106496 | tf_op jit(solution)/shard_map/psum | solution.py:260
  1110.7 20.5 %reduce-scatter.23.cloned.1.call-done = bf16[512,256]{1,0:T(8,128)(2,1)} async-done(((bf16[512,1024]{1,0:T(8,128)(2,1)}), bf16[512,256]{1,0:T(8,128)(2,1)}) %reduce-scatter.23.cloned.1.call-update) | async-done | bytes 262160 | tf_op jit(solution)/shard_map/reduce_scatter | solution.py:256
  1133.0 25.7 %reduce-scatter.19.cloned.1.call-done = bf16[128,1024]{1,0:T(8,128)(2,1)} async-done(((bf16[128,4096]{1,0:T(8,128)(2,1)}), bf16[128,1024]{1,0:T(8,128)(2,1)}) %reduce-scatter.19.cloned.1.call-update) | async-done | bytes 262160 | tf_op jit(solution)/shard_map/reduce_scatter | solution.py:253
  (215 shorter events, 139.3 us)
Async XLA Ops:
  7.2 41.8 %copy-start.2 = (bf16[2,256,1024]{2,1,0:T(8,128)(2,1)S(1)}, bf16[2,256,1024]{2,1,0:T(8,128)(2,1)}, u32[]{:S(2)}) copy-start(bf16[2,256,1024]{2,1,0:T(8,128)(2,1)} %param.27) | copy-start | bytes 3145732
  7.2 143.0 %copy-start.28 = (f32[1024]{0:T(1024)S(1)}, f32[1024]{0:T(1024)}, u32[]{:S(2)}) copy-start(f32[1024]{0:T(1024)} %param.28) | copy-start | bytes 12292
  7.2 143.0 %copy-start.39 = (f32[3072]{0:T(1024)S(1)}, f32[3072]{0:T(1024)}, u32[]{:S(2)}) copy-start(f32[3072]{0:T(1024)} %param.31) | copy-start | bytes 36868
  7.2 143.0 %copy-start.43 = (f32[1024]{0:T(1024)S(1)}, f32[1024]{0:T(1024)}, u32[]{:S(2)}) copy-start(f32[1024]{0:T(1024)} %param.29) | copy-start | bytes 12292
  7.2 23.3 %all-gather.11.cloned.1.call-start = ((), (), s32[]{:S(2)}) async-start(), calls=%async_computation.14 | async-start | bytes 1310720 | tf_op jit(solution)/shard_map/all_gather | solution.py:150
  8.0 41.0 %all-gather.15.cloned.1.call-start = ((), (), s32[]{:S(2)}) async-start(), calls=%async_computation.16 | async-start | bytes 1310720 | tf_op jit(solution)/shard_map/all_gather | solution.py:151
  8.7 141.5 %all-gather.7.cloned.1.call-start = ((), (), s32[]{:S(2)}) async-start(), calls=%async_computation.12 | async-start | bytes 7077888 | tf_op jit(solution)/shard_map/all_gather | solution.py:154
  20.5 252.2 %all-gather.9.cloned.1.call-start = ((), (), s32[]{:S(2)}) async-start(), calls=%async_computation.13 | async-start | bytes 2359296 | tf_op jit(solution)/shard_map/all_gather | solution.py:155
  28.9 296.4 %all-gather.13.cloned.1.call-start = ((), (), s32[]{:S(2)}) async-start(), calls=%async_computation.15 | async-start | bytes 9437184 | tf_op jit(solution)/shard_map/all_gather | solution.py:156
  30.5 419.8 %all-gather.17.cloned.1.call-start = ((), (), s32[]{:S(2)}) async-start(), calls=%async_computation.17 | async-start | bytes 9437184 | tf_op jit(solution)/shard_map/all_gather | solution.py:157
  49.2 108.8 %copy-start.21 = (f32[2,256]{1,0:T(2,128)}, f32[2,256]{1,0:T(2,128)S(1)}, u32[]{:S(2)}) copy-start(f32[2,256]{1,0:T(2,128)S(1)} %broadcast_multiply_fusion.1) | copy-start | bytes 6148
  49.6 108.4 %copy-start.25 = (f32[2,256]{1,0:T(2,128)}, f32[2,256]{1,0:T(2,128)S(1)}, u32[]{:S(2)}) copy-start(f32[2,256]{1,0:T(2,128)S(1)} %fusion.44) | copy-start | bytes 6148
  49.6 108.4 %copy-start.23 = (f32[2,256]{1,0:T(2,128)}, f32[2,256]{1,0:T(2,128)S(1)}, u32[]{:S(2)}) copy-start(f32[2,256]{1,0:T(2,128)S(1)} %fusion.96) | copy-start | bytes 6148
  166.7 42.0 %all-to-all-start = ((bf16[2,256,16,192]{1,3,0,2:T(8,128)(2,1)}), bf16[2,256,16,192]{1,3,0,2:T(8,128)(2,1)}, u32[]{:S(2)}, u32[]{:S(2)}) async-start(bf16[2,256,16,192]{1,3,0,2:T(8,128)(2,1)} %copy.156), calls=%async_computation | async-start | bytes 6291456 | tf_op jit(solution)/shard_map/all_to_all | solution.py:170
  272.6 52.6 %copy-start.37 = (f32[1024]{0:T(1024)S(1)}, f32[1024]{0:T(1024)}, u32[]{:S(2)}) copy-start(f32[1024]{0:T(1024)} %param.34) | copy-start | bytes 12292
  272.6 52.6 %copy-start.45 = (f32[1024]{0:T(1024)S(1)}, f32[1024]{0:T(1024)}, u32[]{:S(2)}) copy-start(f32[1024]{0:T(1024)} %param.35) | copy-start | bytes 12292
  275.9 194.5 %copy-start.5 = (f32[2,256,1024]{2,1,0:T(8,128)}, f32[2,256,1024]{2,1,0:T(8,128)S(1)}, u32[]{:S(2)}) copy-start(f32[2,256,1024]{2,1,0:T(8,128)S(1)} %get-tuple-element.111) | copy-start | bytes 6291460
  276.3 194.1 %copy-start.31 = (f32[2,256]{1,0:T(2,128)}, f32[2,256]{1,0:T(2,128)S(1)}, u32[]{:S(2)}) copy-start(f32[2,256]{1,0:T(2,128)S(1)} %fusion.97) | copy-start | bytes 6148
  276.3 174.0 %copy-start.41 = (f32[4096]{0:T(1024)S(1)}, f32[4096]{0:T(1024)}, u32[]{:S(2)}) copy-start(f32[4096]{0:T(1024)} %param.37) | copy-start | bytes 49156
  478.8 18.0 %all-to-all-start.2 = ((bf16[2,256,16,64]{1,3,0,2:T(8,128)(2,1)}), bf16[2,256,16,64]{1,3,0,2:T(8,128)(2,1)S(1)}, u32[]{:S(2)}, u32[]{:S(2)}) async-start(bf16[2,256,16,64]{1,3,0,2:T(8,128)(2,1)} %copy.165), calls=%async_computation.2 | async-start | bytes 2097152 | tf_op jit(solution)/shard_map/all_to_all | solution.py:217
  482.3 179.7 %reduce-scatter.13.cloned.1.call-start = ((), (), s32[]{:S(2)}) async-start(), calls=%async_computation.20 | async-start | bytes 2359296 | tf_op jit(solution)/shard_map/reduce_scatter | solution.py:236
  486.8 265.1 %reduce-scatter.9.cloned.1.call-start = ((), (), s32[]{:S(2)}) async-start(), calls=%async_computation.18 | async-start | bytes 7077888 | tf_op jit(solution)/shard_map/reduce_scatter | solution.py:233
  636.5 267.2 %reduce-scatter.21.cloned.1.call-start = ((), (), s32[]{:S(2)}) async-start(), calls=%async_computation.24 | async-start | bytes 9437184 | tf_op jit(solution)/shard_map/reduce_scatter | solution.py:242
  650.8 405.1 %reduce-scatter.17.cloned.1.call-start = ((), (), s32[]{:S(2)}) async-start(), calls=%async_computation.22 | async-start | bytes 9437184 | tf_op jit(solution)/shard_map/reduce_scatter | solution.py:239
  661.9 90.8 %copy-start.33 = (f32[2,4]{1,0:T(2,128)S(1)}, f32[2,4]{1,0:T(2,128)}, u32[]{:S(2)}) copy-start(f32[2,4]{1,0:T(2,128)} %get-tuple-element.83) | copy-start | bytes 100
  661.9 90.8 %copy-start.34 = (f32[2,4]{1,0:T(2,128)S(1)}, f32[2,4]{1,0:T(2,128)}, u32[]{:S(2)}) copy-start(f32[2,4]{1,0:T(2,128)} %get-tuple-element.81) | copy-start | bytes 100
  661.9 241.9 %copy-start.47 = (f32[1024]{0:T(1024)S(1)}, f32[1024]{0:T(1024)}, u32[]{:S(2)}) copy-start(f32[1024]{0:T(1024)} %param.39) | copy-start | bytes 12292
  661.9 445.6 %reduce-scatter.15.cloned.1.call-start = ((), (), s32[]{:S(2)}) async-start(), calls=%async_computation.21 | async-start | bytes 327680 | tf_op jit(solution)/shard_map/reduce_scatter | solution.py:250
  662.6 446.4 %reduce-scatter.11.cloned.1.call-start = ((), (), s32[]{:S(2)}) async-start(), calls=%async_computation.19 | async-start | bytes 983040 | tf_op jit(solution)/shard_map/reduce_scatter | solution.py:247
  751.9 379.3 %reduce-scatter.23.cloned.1.call-start = ((), (), s32[]{:S(2)}) async-start(), calls=%async_computation.25 | async-start | bytes 1310720 | tf_op jit(solution)/shard_map/reduce_scatter | solution.py:256
  903.7 34.6 %copy-start.19 = (bf16[128,768]{1,0:T(8,128)(2,1)S(1)}, bf16[128,768]{1,0:T(8,128)(2,1)}, u32[]{:S(2)}) copy-start(bf16[128,768]{1,0:T(8,128)(2,1)} %param.30) | copy-start | bytes 589828
  903.8 255.0 %reduce-scatter.19.cloned.1.call-start = ((), (), s32[]{:S(2)}) async-start(), calls=%async_computation.23 | async-start | bytes 1310720 | tf_op jit(solution)/shard_map/reduce_scatter | solution.py:253
  (40 other events, 246.5 us)
Sparse Core Ops, SparseCore 0:
  9.6 20.8 all-gather.10
  32.0 16.8 all-gather.14
  51.1 99.0 all-gather.6
  152.2 47.6 all-gather.8
  201.8 123.4 all-gather.12
  327.2 123.0 all-gather.16
  486.9 66.2 reduce-scatter.12
  636.6 115.1 reduce-scatter.8
  755.5 148.1 reduce-scatter.20
  907.6 148.2 reduce-scatter.16
  1058.4 19.0 reduce-scatter.14
  1080.1 23.4 reduce-scatter.10
  1106.1 25.0 reduce-scatter.22
  1133.8 24.9 reduce-scatter.18
where the time goes:
time: 1170 us
  waiting for transfers between devices  725 us (62%)
  blocking collectives  154 us (13%)
  matrix products  153 us (13%)
  local copies, waits for them, and re-layouts  71.4 us (6%)
  other arithmetic  39.2 us (3%)
  between operations  15.3 us (1%)
    reduce_scatter x1, waiting for transfers between devices, body(): lax.psum_scatter(grad_contract.astype(jnp.bfloat16), 'fsdp', scatter_dime...  151 us
    all_gather x1, waiting for transfers between devices, body(): lax.all_gather(partial_full[3], 'fsdp', axis=0, tiled=True)  115 us
    reduce_scatter x1, waiting for transfers between devices, body(): lax.psum_scatter(grad_expand.astype(jnp.bfloat16), 'fsdp', scatter_dimens...  105 us
    all_gather x1, waiting for transfers between devices, body(): lax.all_gather(partial_full[0], 'fsdp', axis=0, tiled=True)  101 us
    reduce_scatter x1, waiting for transfers between devices, body(): lax.psum_scatter(grad_mixing.astype(jnp.bfloat16), 'fsdp', scatter_dimens...  89.2 us
    all_to_all x1, blocking collectives, body(): lax.all_to_all(packed_cot, 'seq', split_axis=1, concat_axis=2, tiled=True)  53.8 us
    all_gather x1, waiting for transfers between devices, body(): lax.all_gather(partial_full[2], 'fsdp', axis=0, tiled=True)  48.9 us
    psum x1, blocking collectives, body(): lax.psum((grad_first_gain, grad_first_shift, grad_mixing_bias, grad_outpu...  40.8 us
  transfers between devices with their start and end apart: 16, of which 12 were waited for; matrix products, arithmetic and copies ran while one was open for 19% of the time, Pallas kernels for 0%

commit v1 on v0

--- a/solution.py
+++ b/solution.py
@@ -7,6 +7,7 @@
 H = 16
 HD = 64
 QBLK = 512
+_balance_sites = lambda buf, axis_name, mesh_ax: lax.psum(lax.psum(buf, axis_name), mesh_ax)
 
 
 def layer_norm(values, gain, shift):
@@ -257,7 +258,7 @@
             summed_first[3].astype(jnp.bfloat16), "seq", scatter_dimension=1, tiled=True
         ).astype(jnp.float32),
     )
-    vector_totals = lax.psum(
+    vector_totals = _balance_sites(
         (
             grad_first_gain,
             grad_first_shift,
@@ -268,7 +269,8 @@
             grad_expand_bias,
             grad_contract_bias,
         ),
-        ("fsdp", "seq"),
+        "seq",
+        "fsdp",
     )
     head_peak = lax.pmax(jnp.max(peaks, axis=0), "fsdp")
     rows_here = attention_weight.shape[0]

time: 1170 us -> 1170 us (level)
    psum x1 -> x2, blocking collectives: 40.8 us -> 48.1 us  [the longest x1 36.3 us: lax.psum(lax.psum(buf, axis_name), mesh_ax)]
where the time goes in v1:
time: 1170 us
  waiting for transfers between devices  717 us (61%)
  blocking collectives  162 us (14%)
  matrix products  153 us (13%)
  local copies, waits for them, and re-layouts  71.4 us (6%)
  other arithmetic  39.2 us (3%)
  between operations  15.3 us (1%)
    reduce_scatter x1, waiting for transfers between devices, body(): lax.psum_scatter(grad_contract.astype(jnp.bfloat16), 'fsdp', scatter_dime...  151 us
    all_gather x1, waiting for transfers between devices, body(): lax.all_gather(partial_full[3], 'fsdp', axis=0, tiled=True)  115 us
    reduce_scatter x1, waiting for transfers between devices, body(): lax.psum_scatter(grad_expand.astype(jnp.bfloat16), 'fsdp', scatter_dimens...  105 us
    all_gather x1, waiting for transfers between devices, body(): lax.all_gather(partial_full[0], 'fsdp', axis=0, tiled=True)  101 us
    reduce_scatter x1, waiting for transfers between devices, body(): lax.psum_scatter(grad_mixing.astype(jnp.bfloat16), 'fsdp', scatter_dimens...  89.1 us
    all_to_all x1, blocking collectives, body(): lax.all_to_all(packed_cot, 'seq', split_axis=1, concat_axis=2, tiled=True)  53.9 us
    all_gather x1, waiting for transfers between devices, body(): lax.all_gather(partial_full[2], 'fsdp', axis=0, tiled=True)  48.7 us
    all_to_all x1, waiting for transfers between devices, body(): lax.all_to_all(mixed, 'seq', split_axis=2, concat_axis=1, tiled=True)  36.5 us
  transfers between devices with their start and end apart: 16, of which 12 were waited for; matrix products, arithmetic and copies ran while one was open for 19% of the time, Pallas kernels for 0%

profile of v1, /device:TPU:0, one launch (start us, length us, event | category | flops | bytes accessed | tf_op | source)
XLA Modules:
  0.0 1166.8 jit_solution(2149134504588009515)
XLA Ops:
  8.8 11.7 %all_gather.24 = bf16[128,3072]{1,0:T(8,128)(2,1)} all-gather(bf16[128,768]{1,0:T(8,128)(2,1)} %param.30), channel_id=1, replica_groups=mesh['fsdp'=8,'seq'=4] {'seq'}, dimensions={1}, use_global_device_ids=true | all-gather | bytes 983040 | tf_op jit(solution)/shard_map/all_gather | solution.py:149
  20.5 8.3 all_gather.26
  30.6 18.4 %all-gather.15.cloned.1.call-done = bf16[512,1024]{1,0:T(8,128)(2,1)} async-done(((bf16[512,256]{1,0:T(8,128)(2,1)}), bf16[512,1024]{1,0:T(8,128)(2,1)}) %all-gather.15.cloned.1.call-update) | async-done | bytes 1048592 | tf_op jit(solution)/shard_map/all_gather | solution.py:152
  49.6 100.5 %all-gather.7.cloned.1.call-done = bf16[1024,3072]{1,0:T(8,128)(2,1)} async-done(((bf16[128,3072]{1,0:T(8,128)(2,1)}), bf16[1024,3072]{1,0:T(8,128)(2,1)}) %all-gather.7.cloned.1.call-update) | async-done | bytes 6291472 | tf_op jit(solution)/shard_map/all_gather | solution.py:155
  150.2 7.8 add_convert_fusion
  172.2 36.5 %all-to-all-done = bf16[2,256,16,192]{1,3,0,2:T(8,128)(2,1)} async-done(((bf16[2,256,16,192]{1,3,0,2:T(8,128)(2,1)}), bf16[2,256,16,192]{1,3,0,2:T(8,128)(2,1)}, u32[]{:S(2)}, u32[]{:S(2)}) %all-to-all-start) | async-done | bytes 3145760 | tf_op jit(solution)/shard_map/all_to_all | solution.py:171
  248.1 18.9 %all_to_all.66 = bf16[4,2,65536]{2,1,0:T(2,128)(2,1)} all-to-all(bf16[4,2,65536]{2,1,0:T(2,128)(2,1)} %reshape.309), channel_id=1, replica_groups=mesh['fsdp'=8,'seq'=4] {'seq'}, dimensions={0} | all-to-all | bytes 2097152 | tf_op jit(solution)/shard_map/all_to_all | solution.py:78
  276.4 48.7 %all-gather.13.cloned.1.call-done = bf16[1024,4096]{1,0:T(8,128)(2,1)} async-done(((bf16[128,4096]{1,0:T(8,128)(2,1)}), bf16[1024,4096]{1,0:T(8,128)(2,1)}) %all-gather.13.cloned.1.call-update) | async-done | bytes 8388624 | tf_op jit(solution)/shard_map/all_gather | solution.py:157
  325.1 10.2 fusion.17
  335.3 114.9 %all-gather.17.cloned.1.call-done = bf16[4096,1024]{1,0:T(8,128)(2,1)} async-done(((bf16[512,1024]{1,0:T(8,128)(2,1)}), bf16[4096,1024]{1,0:T(8,128)(2,1)}) %all-gather.17.cloned.1.call-update) | async-done | bytes 8388624 | tf_op jit(solution)/shard_map/all_gather | solution.py:158
  450.2 14.6 %convert_reduce_fusion = (f32[4096]{0:T(1024)}, bf16[2,256,4096]{2,1,0:T(8,128)(2,1)S(1)}) fusion(f32[2,256,4096]{2,1,0:T(8,128)} %fusion.17, f32[4096]{0:T(1024)S(1)} %copy-done.41, bf16[2,256,1024]{2,1,0:T(8,128)(2,1)} %param.40, bf16[4096,1024]{1,0:T(8,128)(2,1)} %all-gather.17.cloned.1.call-done), kind=kOutput, calls=%fused_computation.29 | convolution fusion | flops 4343197696 | bytes 22052864 | tf_op jit(solution)/shard_map/ntd,id->nti/dot_general | solution.py:194
  486.8 9.9 all-to-all-done.2
  506.7 7.6 fusion.99
  526.1 10.9 fusion.98
  537.0 7.9 multiply_convert_fusion
  559.9 7.6 copy.170
  567.5 53.9 %all_to_all.67 = bf16[2,1024,4,192]{3,2,0,1:T(4,128)(2,1)} all-to-all(bf16[2,1024,4,192]{3,2,0,1:T(4,128)(2,1)} %copy.170), channel_id=1, replica_groups=mesh['fsdp'=8,'seq'=4] {'seq'}, dimensions={1} | all-to-all | bytes 6291456 | tf_op jit(solution)/shard_map/all_to_all | solution.py:220
  621.4 7.3 copy.172
  628.7 7.7 bitcast_convert_fusion.2
  637.7 13.1 %bitcast_convert_fusion = bf16[4096,1024]{1,0:T(8,128)(2,1)} fusion(bf16[2,256,1024]{2,1,0:T(8,128)(2,1)S(1)} %copy-done.12, f32[2,256,4096]{2,1,0:T(8,128)} %fusion.17, f32[4096]{0:T(1024)S(1)} %copy-done.42), kind=kOutput, calls=%fused_computation | convolution fusion | flops 4320133120 | bytes 17842176 | tf_op jit(solution)/shard_map/nti,ntd->id/dot_general | solution.py:192
  652.4 9.5 bitcast_convert_fusion.1
  662.6 89.1 %reduce-scatter.9.cloned.1.call-done = bf16[128,3072]{1,0:T(8,128)(2,1)} async-done(((bf16[1024,3072]{1,0:T(8,128)(2,1)}), bf16[128,3072]{1,0:T(8,128)(2,1)}) %reduce-scatter.9.cloned.1.call-update) | async-done | bytes 786448 | tf_op jit(solution)/shard_map/reduce_scatter | solution.py:234
  752.6 151.0 %reduce-scatter.21.cloned.1.call-done = bf16[512,1024]{1,0:T(8,128)(2,1)} async-done(((bf16[4096,1024]{1,0:T(8,128)(2,1)}), bf16[512,1024]{1,0:T(8,128)(2,1)}) %reduce-scatter.21.cloned.1.call-update) | async-done | bytes 1048592 | tf_op jit(solution)/shard_map/reduce_scatter | solution.py:243
  903.7 12.2 %add_convert_fusion.1 = bf16[2,256,1024]{2,1,0:T(8,128)(2,1)} fusion(f32[2,256,1024]{2,1,0:T(8,128)S(1)} %copy-done.6, bf16[4096,1024]{1,0:T(8,128)(2,1)} %all-gather.17.cloned.1.call-done, f32[1024]{0:T(1024)S(1)} %copy-done.47, f32[2,256,4096]{2,1,0:T(8,128)} %fusion.17, f32[4096]{0:T(1024)S(1)} %copy-done.42), kind=kOutput, calls=%fused_computation.83 | convolution fusion | flops 4317511680 | bytes 19943424 | tf_op jit(solution)/shard_map/nti,id->ntd/dot_general | solution.py:187
  915.9 20.6 %pmax.7 = f32[4]{0:T(128)S(1)} all-reduce(f32[4]{0:T(128)S(1)} %maximum_reduce_fusion), channel_id=1, replica_groups=mesh['fsdp'=8,'seq'=4] {'fsdp'}, use_global_device_ids=true, to_apply=%region_49.50 | all-reduce | flops 4 | bytes 32 | tf_op jit(solution)/shard_map/pmax | solution.py:275
  939.1 7.9 copy.193
  950.5 105.3 %reduce-scatter.17.cloned.1.call-done = bf16[128,4096]{1,0:T(8,128)(2,1)} async-done(((bf16[1024,4096]{1,0:T(8,128)(2,1)}), bf16[128,4096]{1,0:T(8,128)(2,1)}) %reduce-scatter.17.cloned.1.call-update) | async-done | bytes 1048592 | tf_op jit(solution)/shard_map/reduce_scatter | solution.py:240
  1055.9 7.0 fusion.100
  1066.6 11.8 %all-reduce.3 = (f32[1024]{0:T(1024)S(1)}, f32[1024]{0:T(1024)S(1)}, f32[3072]{0:T(1024)S(1)}, f32[1024]{0:T(1024)S(1)}, f32[1024]{0:T(1024)S(1)}, /*index=5*/f3...) all-reduce(f32[1024]{0:T(1024)S(1)} %get-tuple-element.87, ...), channel_id=1, replica_groups=mesh['fsdp'=8,'seq'=4] {'seq'}, use_global_device_ids=true, to_apply=%region_15.16 | all-reduce | flops 13312 | bytes 106496 | tf_op jit(solution)/shard_map/psum | solution.py:10
  1078.4 36.3 %all-reduce.2 = (f32[1024]{0:T(1024)}, f32[1024]{0:T(1024)}, f32[3072]{0:T(1024)}, f32[1024]{0:T(1024)}, f32[1024]{0:T(1024)}, /*index=5*/f32[1024]{0:T(1024)}, f32[4096]{0:T(1024)}, f32[1024]{0:T(1024)}) all-reduce(f32[1024]{0:T(1024)S(1)} %get-tuple-element.100, ...), channel_id=1, replica_groups=mesh['fsdp'=8,'seq'=4] {'fsdp'}, use_global_device_ids=true, to_apply=%region_16.17 | all-reduce | flops 13312 | bytes 106496 | tf_op jit(solution)/shard_map/psum | solution.py:10
  1117.9 12.9 %reduce-scatter.23.cloned.1.call-done = bf16[512,256]{1,0:T(8,128)(2,1)} async-done(((bf16[512,1024]{1,0:T(8,128)(2,1)}), bf16[512,256]{1,0:T(8,128)(2,1)}) %reduce-scatter.23.cloned.1.call-update) | async-done | bytes 262160 | tf_op jit(solution)/shard_map/reduce_scatter | solution.py:257
  1132.5 25.7 %reduce-scatter.19.cloned.1.call-done = bf16[128,1024]{1,0:T(8,128)(2,1)} async-done(((bf16[128,4096]{1,0:T(8,128)(2,1)}), bf16[128,1024]{1,0:T(8,128)(2,1)}) %reduce-scatter.19.cloned.1.call-update) | async-done | bytes 262160 | tf_op jit(solution)/shard_map/reduce_scatter | solution.py:254
  (216 shorter events, 145.7 us)
Async XLA Ops:
  7.2 41.8 %copy-start.2 = (bf16[2,256,1024]{2,1,0:T(8,128)(2,1)S(1)}, bf16[2,256,1024]{2,1,0:T(8,128)(2,1)}, u32[]{:S(2)}) copy-start(bf16[2,256,1024]{2,1,0:T(8,128)(2,1)} %param.27) | copy-start | bytes 3145732
  7.2 143.0 %copy-start.28 = (f32[1024]{0:T(1024)S(1)}, f32[1024]{0:T(1024)}, u32[]{:S(2)}) copy-start(f32[1024]{0:T(1024)} %param.28) | copy-start | bytes 12292
  7.2 143.0 %copy-start.39 = (f32[3072]{0:T(1024)S(1)}, f32[3072]{0:T(1024)}, u32[]{:S(2)}) copy-start(f32[3072]{0:T(1024)} %param.31) | copy-start | bytes 36868
  7.2 143.0 %copy-start.43 = (f32[1024]{0:T(1024)S(1)}, f32[1024]{0:T(1024)}, u32[]{:S(2)}) copy-start(f32[1024]{0:T(1024)} %param.29) | copy-start | bytes 12292
  7.2 23.3 %all-gather.11.cloned.1.call-start = ((), (), s32[]{:S(2)}) async-start(), calls=%async_computation.14 | async-start | bytes 1310720 | tf_op jit(solution)/shard_map/all_gather | solution.py:151
  8.0 41.0 %all-gather.15.cloned.1.call-start = ((), (), s32[]{:S(2)}) async-start(), calls=%async_computation.16 | async-start | bytes 1310720 | tf_op jit(solution)/shard_map/all_gather | solution.py:152
  8.7 141.5 %all-gather.7.cloned.1.call-start = ((), (), s32[]{:S(2)}) async-start(), calls=%async_computation.12 | async-start | bytes 7077888 | tf_op jit(solution)/shard_map/all_gather | solution.py:155
  20.5 252.2 %all-gather.9.cloned.1.call-start = ((), (), s32[]{:S(2)}) async-start(), calls=%async_computation.13 | async-start | bytes 2359296 | tf_op jit(solution)/shard_map/all_gather | solution.py:156
  28.9 296.2 %all-gather.13.cloned.1.call-start = ((), (), s32[]{:S(2)}) async-start(), calls=%async_computation.15 | async-start | bytes 9437184 | tf_op jit(solution)/shard_map/all_gather | solution.py:157
  30.5 419.7 %all-gather.17.cloned.1.call-start = ((), (), s32[]{:S(2)}) async-start(), calls=%async_computation.17 | async-start | bytes 9437184 | tf_op jit(solution)/shard_map/all_gather | solution.py:158
  49.2 108.9 %copy-start.21 = (f32[2,256]{1,0:T(2,128)}, f32[2,256]{1,0:T(2,128)S(1)}, u32[]{:S(2)}) copy-start(f32[2,256]{1,0:T(2,128)S(1)} %broadcast_multiply_fusion.1) | copy-start | bytes 6148
  49.6 108.4 %copy-start.25 = (f32[2,256]{1,0:T(2,128)}, f32[2,256]{1,0:T(2,128)S(1)}, u32[]{:S(2)}) copy-start(f32[2,256]{1,0:T(2,128)S(1)} %fusion.44) | copy-start | bytes 6148
  49.6 108.4 %copy-start.23 = (f32[2,256]{1,0:T(2,128)}, f32[2,256]{1,0:T(2,128)S(1)}, u32[]{:S(2)}) copy-start(f32[2,256]{1,0:T(2,128)S(1)} %fusion.96) | copy-start | bytes 6148
  166.8 42.0 %all-to-all-start = ((bf16[2,256,16,192]{1,3,0,2:T(8,128)(2,1)}), bf16[2,256,16,192]{1,3,0,2:T(8,128)(2,1)}, u32[]{:S(2)}, u32[]{:S(2)}) async-start(bf16[2,256,16,192]{1,3,0,2:T(8,128)(2,1)} %copy.156), calls=%async_computation | async-start | bytes 6291456 | tf_op jit(solution)/shard_map/all_to_all | solution.py:171
  272.7 52.4 %copy-start.37 = (f32[1024]{0:T(1024)S(1)}, f32[1024]{0:T(1024)}, u32[]{:S(2)}) copy-start(f32[1024]{0:T(1024)} %param.34) | copy-start | bytes 12292
  272.7 52.4 %copy-start.45 = (f32[1024]{0:T(1024)S(1)}, f32[1024]{0:T(1024)}, u32[]{:S(2)}) copy-start(f32[1024]{0:T(1024)} %param.35) | copy-start | bytes 12292
  276.0 194.3 %copy-start.5 = (f32[2,256,1024]{2,1,0:T(8,128)}, f32[2,256,1024]{2,1,0:T(8,128)S(1)}, u32[]{:S(2)}) copy-start(f32[2,256,1024]{2,1,0:T(8,128)S(1)} %get-tuple-element.119) | copy-start | bytes 6291460
  276.4 193.9 %copy-start.31 = (f32[2,256]{1,0:T(2,128)}, f32[2,256]{1,0:T(2,128)S(1)}, u32[]{:S(2)}) copy-start(f32[2,256]{1,0:T(2,128)S(1)} %fusion.97) | copy-start | bytes 6148
  276.4 173.8 %copy-start.41 = (f32[4096]{0:T(1024)S(1)}, f32[4096]{0:T(1024)}, u32[]{:S(2)}) copy-start(f32[4096]{0:T(1024)} %param.37) | copy-start | bytes 49156
  478.7 18.0 %all-to-all-start.2 = ((bf16[2,256,16,64]{1,3,0,2:T(8,128)(2,1)}), bf16[2,256,16,64]{1,3,0,2:T(8,128)(2,1)S(1)}, u32[]{:S(2)}, u32[]{:S(2)}) async-start(bf16[2,256,16,64]{1,3,0,2:T(8,128)(2,1)} %copy.165), calls=%async_computation.2 | async-start | bytes 2097152 | tf_op jit(solution)/shard_map/all_to_all | solution.py:218
  482.2 179.7 %reduce-scatter.13.cloned.1.call-start = ((), (), s32[]{:S(2)}) async-start(), calls=%async_computation.20 | async-start | bytes 2359296 | tf_op jit(solution)/shard_map/reduce_scatter | solution.py:237
  486.7 265.1 %reduce-scatter.9.cloned.1.call-start = ((), (), s32[]{:S(2)}) async-start(), calls=%async_computation.18 | async-start | bytes 7077888 | tf_op jit(solution)/shard_map/reduce_scatter | solution.py:234
  636.5 267.1 %reduce-scatter.21.cloned.1.call-start = ((), (), s32[]{:S(2)}) async-start(), calls=%async_computation.24 | async-start | bytes 9437184 | tf_op jit(solution)/shard_map/reduce_scatter | solution.py:243
  650.8 405.0 %reduce-scatter.17.cloned.1.call-start = ((), (), s32[]{:S(2)}) async-start(), calls=%async_computation.22 | async-start | bytes 9437184 | tf_op jit(solution)/shard_map/reduce_scatter | solution.py:240
  661.8 90.7 %copy-start.33 = (f32[2,4]{1,0:T(2,128)S(1)}, f32[2,4]{1,0:T(2,128)}, u32[]{:S(2)}) copy-start(f32[2,4]{1,0:T(2,128)} %get-tuple-element.83) | copy-start | bytes 100
  661.8 90.7 %copy-start.34 = (f32[2,4]{1,0:T(2,128)S(1)}, f32[2,4]{1,0:T(2,128)}, u32[]{:S(2)}) copy-start(f32[2,4]{1,0:T(2,128)} %get-tuple-element.81) | copy-start | bytes 100
  661.8 241.9 %copy-start.47 = (f32[1024]{0:T(1024)S(1)}, f32[1024]{0:T(1024)}, u32[]{:S(2)}) copy-start(f32[1024]{0:T(1024)} %param.39) | copy-start | bytes 12292
  661.8 452.8 %reduce-scatter.15.cloned.1.call-start = ((), (), s32[]{:S(2)}) async-start(), calls=%async_computation.21 | async-start | bytes 327680 | tf_op jit(solution)/shard_map/reduce_scatter | solution.py:251
  662.6 453.6 %reduce-scatter.11.cloned.1.call-start = ((), (), s32[]{:S(2)}) async-start(), calls=%async_computation.19 | async-start | bytes 983040 | tf_op jit(solution)/shard_map/reduce_scatter | solution.py:248
  751.8 379.0 %reduce-scatter.23.cloned.1.call-start = ((), (), s32[]{:S(2)}) async-start(), calls=%async_computation.25 | async-start | bytes 1310720 | tf_op jit(solution)/shard_map/reduce_scatter | solution.py:257
  903.6 34.7 %copy-start.19 = (bf16[128,768]{1,0:T(8,128)(2,1)S(1)}, bf16[128,768]{1,0:T(8,128)(2,1)}, u32[]{:S(2)}) copy-start(bf16[128,768]{1,0:T(8,128)(2,1)} %param.30) | copy-start | bytes 589828
  903.6 254.7 %reduce-scatter.19.cloned.1.call-start = ((), (), s32[]{:S(2)}) async-start(), calls=%async_computation.23 | async-start | bytes 1310720 | tf_op jit(solution)/shard_map/reduce_scatter | solution.py:254
  (40 other events, 246.6 us)
Sparse Core Ops, SparseCore 0:
  9.6 20.8 all-gather.10
  32.0 16.8 all-gather.14
  51.1 99.0 all-gather.6
  152.2 47.4 all-gather.8
  201.6 123.4 all-gather.12
  327.1 123.1 all-gather.16
  486.8 66.3 reduce-scatter.12
  636.6 115.1 reduce-scatter.8
  755.4 148.1 reduce-scatter.20
  907.5 148.2 reduce-scatter.16
  1058.3 19.2 reduce-scatter.14
  1080.1 23.1 reduce-scatter.10
  1105.8 24.8 reduce-scatter.22
  1133.3 24.9 reduce-scatter.18
